TPU v7x, 256 devices: a whole 4x4x8 slice. The times are simulated.
256 devices in a mesh: grp: 32 (over x_hi, z, core), rep: 8 (over x_lo, y).
Axes of the slice: x: 4 (x_hi: 2, x_lo: 2; x = x_hi * 2 + x_lo), y: 4, z: 8, core: 2. Of those that a mesh axis runs over, the one named last changes fastest.
Arguments:
- features: bfloat16 [24576, 512], P(('grp', 'rep')), may hold values from -6 to 6
- tile_values: bfloat16 [768, 32, 2, 128, 128], P(('grp', 'rep')), may hold values from 0.019897461 to 1
- tile_columns: int32 [768, 32, 2], P(('grp', 'rep')), may hold values from 0 to 5, as said below
- tile_counts: int32 [768, 32], P(('grp', 'rep')), may hold values from 0 to 2
- state_ids: int32 [98304], P(('grp', 'rep')), may hold values from 0 to 24575
- self_weight: bfloat16 [512, 512], replicated, may hold values from -0.25 to 0.25
- neighbour_weight: bfloat16 [512, 512], replicated, may hold values from -0.25 to 0.25
- bias_vector: float32 [512], replicated, may hold values from -3 to 3
Outputs:
- embedded: bfloat16 [98304, 512], P(('grp', 'rep'))
Inputs may be any that keep to these rules, and one draw needn't show every extreme that they name: `tile_columns`: for each row block and group the first tile_counts entries name distinct column blocks of that group; entries beyond the count are padding and are ignored.
All inputs are finite; a program needn't handle non-finite values.
Results may differ from a plain program's by a relative error of at most 0.0033.
Values may be sent and summed in bfloat16 or wider, within the bound.
A program may use at most 192 MiB of HBM per device.

v0:
```python
import jax
import jax.numpy as jnp
from jax import lax
from jax.sharding import PartitionSpec as P


def on_device(
    features,
    tile_values,
    tile_columns,
    tile_counts,
    state_ids,
    self_weight,
    neighbour_weight,
    bias_vector,
):
    panels = lax.all_gather(features, "rep", axis=0, tiled=True)
    row_blocks = tile_values.shape[0]
    group_count = tile_values.shape[1]
    slot_count = tile_values.shape[2]
    tile_size = tile_values.shape[3]
    panel_rows = panels.shape[0]
    width = panels.shape[1]
    panel_blocks = panel_rows // tile_size
    local_rows = row_blocks * tile_size
    positions = lax.broadcasted_iota(jnp.int32, (row_blocks, group_count, slot_count), 2)
    usable = positions < tile_counts[:, :, None]
    row_sums = jnp.sum(tile_values, axis=4, dtype=jnp.float32)
    degree = 1.0 + jnp.sum(
        jnp.where(usable[:, :, :, None], row_sums, jnp.float32(0.0)), axis=(1, 2)
    ).reshape(local_rows)
    masked_values = jnp.where(usable[:, :, :, None, None], tile_values, jnp.zeros((), jnp.bfloat16))
    block_iota = lax.broadcasted_iota(jnp.int32, (1, 1, panel_blocks), 2)
    zero_value = jnp.zeros((), jnp.bfloat16)

    def dense_group(group):
        columns = lax.dynamic_index_in_dim(tile_columns, group, 1, keepdims=False)
        values = lax.dynamic_index_in_dim(masked_values, group, 1, keepdims=False)
        hits = columns[:, :, None] == block_iota
        dense = jnp.zeros((row_blocks, tile_size, panel_blocks, tile_size), jnp.bfloat16)
        for slot in range(slot_count):
            placed = jnp.where(
                hits[:, slot, None, :, None], values[:, slot, :, None, :], zero_value
            )
            dense = dense + placed
        return dense.reshape(local_rows, panel_rows)

    def group_product(window, group, totals):
        dense = dense_group(group)
        return totals + jnp.dot(dense, window, preferred_element_type=jnp.float32)

    everything = lax.all_gather(panels, "grp", axis=0, tiled=True)

    def each_group(group, running):
        window = lax.dynamic_slice_in_dim(everything, group * panel_rows, panel_rows, 0)
        return group_product(window, group, running)

    totals = lax.fori_loop(0, group_count, each_group, jnp.zeros((local_rows, width), jnp.float32))
    own_rows = jnp.take(everything, state_ids, axis=0)
    neighbour = (totals / jnp.sqrt(degree)[:, None]).astype(jnp.bfloat16)
    activation = jnp.dot(own_rows, self_weight, preferred_element_type=jnp.float32)
    activation = activation + jnp.dot(
        neighbour, neighbour_weight, preferred_element_type=jnp.float32
    )
    activation = activation + bias_vector[None, :]
    return jnp.maximum(activation, 0.0).astype(jnp.bfloat16)


def solution(mesh):
    placed = (
        P(("grp", "rep"), None),
        P(("grp", "rep"), None, None, None, None),
        P(("grp", "rep"), None, None),
        P(("grp", "rep"), None),
        P(("grp", "rep")),
        P(),
        P(),
        P(),
    )
    return jax.shard_map(
        on_device, mesh=mesh, in_specs=placed, out_specs=P(("grp", "rep"), None), check_vma=False
    )
```

profile of v0, /device:TPU:1, one launch (start us, length us, event | category | flops | bytes accessed | tf_op | source)
XLA Modules:
  0.0 342.0 jit_solution(12657822559184209282)
XLA Ops:
  6.5 27.6 %all_gather.6 = bf16[768,512]{1,0:T(8,128)(2,1)} all-gather(bf16[96,512]{1,0:T(8,128)(2,1)} %param.10), channel_id=1, replica_groups=mesh['grp'=32,'rep'=8] {'rep'}, dimensions={0}, use_global_device_ids=true | all-gather | bytes 884736 | tf_op jit(solution)/shard_map/all_gather | solution.py:17
  36.9 4.7 %convert_reduce_fusion = f32[3,32,2,128]{3,2,1,0:T(2,128)S(1)} fusion(bf16[3,32,2,128,128]{4,3,2,1,0:T(8,128)(2,1)} %param.11), kind=kLoop, calls=%fused_computation.15 | loop fusion | flops 6266880 | bytes 6389760 | tf_op jit(solution)/shard_map/reduce_sum | solution.py:28
  41.9 3.1 copy_select_fusion
  44.9 178.6 %all-gather.2.cloned.1.call-done = bf16[24576,512]{1,0:T(8,128)(2,1)} async-done(((bf16[768,512]{1,0:T(8,128)(2,1)}), bf16[24576,512]{1,0:T(8,128)(2,1)}) %all-gather.2.cloned.1.call-update) | async-done | bytes 25165840 | tf_op jit(solution)/shard_map/all_gather | solution.py:52
  223.6 96.5 %while.14 = (s32[]{:T(128)}, f32[384,512]{1,0:T(8,128)S(1)}, s32[3,32,2]{0,2,1:T(2,128)S(1)}, bf16[3,32,2,128,128]{4,3,0,2,1:T(8,128)(2,1)}, bf16[24576,512]{1,0...) while((s32[]{:T(128)}, f32[384,512]{1,0:T(8,128)S(1)}, ...), condition=%wide.region_1.2_spmd.clone, body=%wide.region_0.0_spmd.clone.sunk | while | flops 303267872 | bytes 4522361 | solution.py:58
  223.6 1.0 dynamic-slice_bitcast_fusion.5
  224.9 1.7 convolution_add_fusion.3
  226.6 0.9 dynamic-slice_bitcast_fusion.5
  227.9 1.7 convolution_add_fusion.3
  229.6 0.9 dynamic-slice_bitcast_fusion.5
  231.0 1.7 convolution_add_fusion.3
  232.7 0.9 dynamic-slice_bitcast_fusion.5
  234.0 1.7 convolution_add_fusion.3
  235.7 0.9 dynamic-slice_bitcast_fusion.5
  237.0 1.7 convolution_add_fusion.3
  238.7 0.9 dynamic-slice_bitcast_fusion.5
  240.0 1.7 convolution_add_fusion.3
  241.7 0.9 dynamic-slice_bitcast_fusion.5
  243.0 1.7 convolution_add_fusion.3
  244.7 0.9 dynamic-slice_bitcast_fusion.5
  246.0 1.7 convolution_add_fusion.3
  247.7 0.9 dynamic-slice_bitcast_fusion.5
  249.1 1.7 convolution_add_fusion.3
  250.7 0.9 dynamic-slice_bitcast_fusion.5
  252.1 1.7 convolution_add_fusion.3
  253.8 0.9 dynamic-slice_bitcast_fusion.5
  255.1 1.7 convolution_add_fusion.3
  256.8 0.9 dynamic-slice_bitcast_fusion.5
  258.1 1.7 convolution_add_fusion.3
  259.8 0.9 dynamic-slice_bitcast_fusion.5
  261.1 1.7 convolution_add_fusion.3
  262.8 0.9 dynamic-slice_bitcast_fusion.5
  264.1 1.7 convolution_add_fusion.3
  265.8 0.9 dynamic-slice_bitcast_fusion.5
  267.1 1.7 convolution_add_fusion.3
  268.8 0.9 dynamic-slice_bitcast_fusion.5
  270.2 1.7 convolution_add_fusion.3
  271.8 0.9 dynamic-slice_bitcast_fusion.5
  273.2 1.7 convolution_add_fusion.3
  274.9 0.9 dynamic-slice_bitcast_fusion.5
  276.2 1.7 convolution_add_fusion.3
  277.9 0.9 dynamic-slice_bitcast_fusion.5
  279.2 1.7 convolution_add_fusion.3
  280.9 0.9 dynamic-slice_bitcast_fusion.5
  282.2 1.7 convolution_add_fusion.3
  285.2 1.7 convolution_add_fusion.3
  288.2 1.7 convolution_add_fusion.3
  291.3 1.7 convolution_add_fusion.3
  292.9 0.9 dynamic-slice_bitcast_fusion.5
  294.3 1.7 convolution_add_fusion.3
  297.3 1.7 convolution_add_fusion.3
  299.0 0.9 dynamic-slice_bitcast_fusion.5
  300.3 1.7 convolution_add_fusion.3
  302.0 0.9 dynamic-slice_bitcast_fusion.5
  303.3 1.7 convolution_add_fusion.3
  306.3 1.7 convolution_add_fusion.3
  308.0 0.9 dynamic-slice_bitcast_fusion.5
  309.3 1.7 convolution_add_fusion.3
  312.4 1.7 convolution_add_fusion.3
  314.1 0.9 dynamic-slice_bitcast_fusion.5
  315.4 1.7 convolution_add_fusion.3
  318.4 1.7 convolution_add_fusion.3
  320.1 13.5 %gather_fusion = bf16[384,512]{1,0:T(8,128)(2,1)S(1)} fusion(bf16[24576,512]{1,0:T(8,128)(2,1)} %get-tuple-element.239, s32[1024]{0:T(1024)S(1)} %pad_clamp_fusion), kind=kCustom, calls=%fused_computation | custom fusion | bytes 787968 | tf_op jit(solution)/shard_map/jit(_take)/gather | solution.py:59
  334.0 1.2 fusion.8
  (189 shorter events, 21.0 us)
Async XLA Ops:
  6.5 327.0 %copy-start = (bf16[512,512]{1,0:T(8,128)(2,1)S(1)}, bf16[512,512]{1,0:T(8,128)(2,1)}, u32[]{:S(2)}) copy-start(bf16[512,512]{1,0:T(8,128)(2,1)} %param.15) | copy-start | bytes 1572868
  6.5 35.3 %copy-start.2 = (s32[384]{0:T(512)S(1)}, s32[384]{0:T(512)}, u32[]{:S(2)}) copy-start(s32[384]{0:T(512)} %param.14) | copy-start | bytes 4612
  6.5 217.0 %all-gather.2.cloned.1.call-start = ((), (), s32[]{:S(2)}) async-start(), calls=%async_computation | async-start | bytes 25952256 | tf_op jit(solution)/shard_map/all_gather | solution.py:52
  36.1 5.8 %copy-start.1 = (bf16[3,32,2,128,128]{4,3,2,1,0:T(8,128)(2,1)S(1)}, bf16[3,32,2,128,128]{4,3,2,1,0:T(8,128)(2,1)}, u32[]{:S(2)}) copy-start(bf16[3,32,2,128,128]{4,3,2,1,0:T(8,128)(2,1)} %param.11) | copy-start | bytes 18874372
  223.6 110.4 %copy-start.3 = (bf16[512,512]{1,0:T(8,128)(2,1)S(1)}, bf16[512,512]{1,0:T(8,128)(2,1)}, u32[]{:S(2)}) copy-start(bf16[512,512]{1,0:T(8,128)(2,1)} %param.16) | copy-start | bytes 1572868
  223.6 110.4 %copy-start.4 = (f32[512]{0:T(512)S(1)}, f32[512]{0:T(512)}, u32[]{:S(2)}) copy-start(f32[512]{0:T(512)} %param.17) | copy-start | bytes 6148
Sparse Core Ops, SparseCore 0:
  34.3 189.1 all-gather.1
where the time goes:
time: 344 us; the launch traced here: 342 us
  waiting for transfers between devices  179 us (52%)
  matrix products  54.9 us (16%)
  local copies, waits for them, and re-layouts  45.8 us (13%)
  blocking collectives  27.6 us (8%)
  other arithmetic  19.7 us (6%)
  between operations  13.5 us (4%)
    all_gather x1, waiting for transfers between devices, on_device(): everything = lax.all_gather(panels, 'grp', axis=0, tiled=True)  179 us
    dot_general x32, matrix products, group_product(): return totals + jnp.dot(dense, window, preferred_element_type=jnp.float32)  53.3 us
    squeeze x32, local copies, waits for them, and re-layouts, dense_group(): values = lax.dynamic_index_in_dim(masked_values, group, 1, keepdims=False)  30.3 us
    all_gather x1, blocking collectives, on_device(): panels = lax.all_gather(features, 'rep', axis=0, tiled=True)  27.6 us
    gather x1, local copies, waits for them, and re-layouts, on_device(): own_rows = jnp.take(everything, state_ids, axis=0)  13.5 us
    add x32, other arithmetic, dense_group(): dense = dense + placed  7.71 us
  transfers between devices with their start and end apart: 1, of which 1 were waited for; matrix products, arithmetic and copies ran while one was open for 3% of the time, Pallas kernels for 0%

commit v1 on v0

--- a/solution.py
+++ b/solution.py
@@ -14,7 +14,9 @@
     neighbour_weight,
     bias_vector,
 ):
-    panels = lax.all_gather(features, "rep", axis=0, tiled=True)
+    panels = jnp.concatenate(
+        lax.all_to_all(jnp.stack([features] * lax.axis_size("rep")), "rep", 0, 0), axis=0
+    )
     row_blocks = tile_values.shape[0]
     group_count = tile_values.shape[1]
     slot_count = tile_values.shape[2]

time: 344 us -> 329 us (0.956)
  blocking collectives: 27.6 us -> 17.3 us
  waiting for transfers between devices: 179 us -> 173 us
    all_gather x1 -> x0, blocking collectives: 27.6 us -> none  [on_device(): panels = lax.all_gather(features, 'rep', axis=0, tiled=True)]
    all_to_all x0 -> x1, blocking collectives: none -> 17.3 us  [on_device(): lax.all_to_all(jnp.stack([features] * lax.axis_size('rep')), 'rep', 0, 0)]
    all_gather x1, waiting for transfers between devices: 179 us -> 173 us  [on_device(): everything = lax.all_gather(panels, 'grp', axis=0, tiled=True)]
where the time goes in v1:
time: 329 us; the launch traced here: 327 us
  waiting for transfers between devices  173 us (53%)
  matrix products  54.9 us (17%)
  local copies, waits for them, and re-layouts  46.9 us (14%)
  other arithmetic  19.7 us (6%)
  blocking collectives  17.3 us (5%)
  between operations  13.5 us (4%)
    all_gather x1, waiting for transfers between devices, on_device(): everything = lax.all_gather(panels, 'grp', axis=0, tiled=True)  173 us
    dot_general x32, matrix products, group_product(): return totals + jnp.dot(dense, window, preferred_element_type=jnp.float32)  53.4 us
    squeeze x32, local copies, waits for them, and re-layouts, dense_group(): values = lax.dynamic_index_in_dim(masked_values, group, 1, keepdims=False)  30.3 us
    all_to_all x1, blocking collectives, on_device(): lax.all_to_all(jnp.stack([features] * lax.axis_size('rep')), 'rep', 0, 0)  17.3 us
    gather x1, local copies, waits for them, and re-layouts, on_device(): own_rows = jnp.take(everything, state_ids, axis=0)  13.5 us
    add x32, other arithmetic, dense_group(): dense = dense + placed  7.71 us
  transfers between devices with their start and end apart: 1, of which 1 were waited for; matrix products, arithmetic and copies ran while one was open for 3% of the time, Pallas kernels for 0%

profile of v1, /device:TPU:1, one launch (start us, length us, event | category | flops | bytes accessed | tf_op | source)
XLA Modules:
  0.0 326.8 jit_solution(13558684867429153303)
XLA Ops:
  6.5 1.0 stack.2
  7.6 17.3 %all_to_all.5 = bf16[8,96,512]{2,1,0:T(8,128)(2,1)} all-to-all(bf16[8,96,512]{2,1,0:T(8,128)(2,1)S(1)} %stack.2), channel_id=1, replica_groups=mesh['grp'=32,'rep'=8] {'rep'}, dimensions={0} | all-to-all | bytes 1572864 | tf_op jit(solution)/shard_map/all_to_all | solution.py:18
  27.6 4.7 %convert_reduce_fusion = f32[3,32,2,128]{3,2,1,0:T(2,128)S(1)} fusion(bf16[3,32,2,128,128]{4,3,2,1,0:T(8,128)(2,1)} %param.11), kind=kLoop, calls=%fused_computation.15 | loop fusion | flops 6266880 | bytes 6389760 | tf_op jit(solution)/shard_map/reduce_sum | solution.py:30
  32.6 3.1 copy_select_fusion
  35.7 172.6 %all-gather.2.cloned.1.call-done = bf16[24576,512]{1,0:T(8,128)(2,1)} async-done(((bf16[768,512]{1,0:T(8,128)(2,1)}), bf16[24576,512]{1,0:T(8,128)(2,1)}) %all-gather.2.cloned.1.call-update) | async-done | bytes 25165840 | tf_op jit(solution)/shard_map/all_gather | solution.py:54
  208.3 96.5 %while.14 = (s32[]{:T(128)}, f32[384,512]{1,0:T(8,128)S(1)}, s32[3,32,2]{0,2,1:T(2,128)S(1)}, bf16[3,32,2,128,128]{4,3,0,2,1:T(8,128)(2,1)}, bf16[24576,512]{1,0...) while((s32[]{:T(128)}, f32[384,512]{1,0:T(8,128)S(1)}, ...), condition=%wide.region_1.2_spmd.clone, body=%wide.region_0.0_spmd.clone.sunk | while | flops 303267872 | bytes 4522361 | solution.py:60
  208.3 1.0 dynamic-slice_bitcast_fusion.5
  209.7 1.7 convolution_add_fusion.3
  211.4 0.9 dynamic-slice_bitcast_fusion.5
  212.7 1.7 convolution_add_fusion.3
  214.4 0.9 dynamic-slice_bitcast_fusion.5
  215.7 1.7 convolution_add_fusion.3
  217.4 0.9 dynamic-slice_bitcast_fusion.5
  218.7 1.7 convolution_add_fusion.3
  220.4 0.9 dynamic-slice_bitcast_fusion.5
  221.8 1.7 convolution_add_fusion.3
  223.4 0.9 dynamic-slice_bitcast_fusion.5
  224.8 1.7 convolution_add_fusion.3
  226.5 0.9 dynamic-slice_bitcast_fusion.5
  227.8 1.7 convolution_add_fusion.3
  229.5 0.9 dynamic-slice_bitcast_fusion.5
  230.8 1.7 convolution_add_fusion.3
  232.5 0.9 dynamic-slice_bitcast_fusion.5
  233.8 1.7 convolution_add_fusion.3
  235.5 0.9 dynamic-slice_bitcast_fusion.5
  236.8 1.7 convolution_add_fusion.3
  238.5 0.9 dynamic-slice_bitcast_fusion.5
  239.8 1.7 convolution_add_fusion.3
  241.5 0.9 dynamic-slice_bitcast_fusion.5
  242.9 1.7 convolution_add_fusion.3
  244.6 0.9 dynamic-slice_bitcast_fusion.5
  245.9 1.7 convolution_add_fusion.3
  247.6 0.9 dynamic-slice_bitcast_fusion.5
  248.9 1.7 convolution_add_fusion.3
  250.6 0.9 dynamic-slice_bitcast_fusion.5
  251.9 1.7 convolution_add_fusion.3
  253.6 0.9 dynamic-slice_bitcast_fusion.5
  254.9 1.7 convolution_add_fusion.3
  256.6 0.9 dynamic-slice_bitcast_fusion.5
  257.9 1.7 convolution_add_fusion.3
  259.6 0.9 dynamic-slice_bitcast_fusion.5
  260.9 1.7 convolution_add_fusion.3
  262.6 0.9 dynamic-slice_bitcast_fusion.5
  264.0 1.7 convolution_add_fusion.3
  265.7 0.9 dynamic-slice_bitcast_fusion.5
  267.0 1.7 convolution_add_fusion.3
  268.7 0.9 dynamic-slice_bitcast_fusion.5
  270.0 1.7 convolution_add_fusion.3
  273.0 1.7 convolution_add_fusion.3
  274.7 0.9 dynamic-slice_bitcast_fusion.5
  276.0 1.7 convolution_add_fusion.3
  279.0 1.7 convolution_add_fusion.3
  280.7 0.9 dynamic-slice_bitcast_fusion.5
  282.1 1.7 convolution_add_fusion.3
  285.1 1.7 convolution_add_fusion.3
  288.1 1.7 convolution_add_fusion.3
  291.1 1.7 convolution_add_fusion.3
  292.8 0.9 dynamic-slice_bitcast_fusion.5
  294.1 1.7 convolution_add_fusion.3
  297.1 1.7 convolution_add_fusion.3
  300.1 1.7 convolution_add_fusion.3
  303.2 1.7 convolution_add_fusion.3
  304.8 13.5 %gather_fusion = bf16[384,512]{1,0:T(8,128)(2,1)S(1)} fusion(bf16[24576,512]{1,0:T(8,128)(2,1)} %get-tuple-element.239, s32[1024]{0:T(1024)S(1)} %pad_clamp_fusion), kind=kCustom, calls=%fused_computation | custom fusion | bytes 787968 | tf_op jit(solution)/shard_map/jit(_take)/gather | solution.py:61
  318.8 1.2 fusion.8
  (190 shorter events, 22.0 us)
Async XLA Ops:
  6.5 311.8 %copy-start = (bf16[512,512]{1,0:T(8,128)(2,1)S(1)}, bf16[512,512]{1,0:T(8,128)(2,1)}, u32[]{:S(2)}) copy-start(bf16[512,512]{1,0:T(8,128)(2,1)} %param.15) | copy-start | bytes 1572868
  6.5 26.0 %copy-start.2 = (s32[384]{0:T(512)S(1)}, s32[384]{0:T(512)}, u32[]{:S(2)}) copy-start(s32[384]{0:T(512)} %param.14) | copy-start | bytes 4612
  6.5 201.8 %all-gather.2.cloned.1.call-start = ((), (), s32[]{:S(2)}) async-start(), calls=%async_computation.1 | async-start | bytes 25952256 | tf_op jit(solution)/shard_map/all_gather | solution.py:54
  26.8 5.8 %copy-start.1 = (bf16[3,32,2,128,128]{4,3,2,1,0:T(8,128)(2,1)S(1)}, bf16[3,32,2,128,128]{4,3,2,1,0:T(8,128)(2,1)}, u32[]{:S(2)}) copy-start(bf16[3,32,2,128,128]{4,3,2,1,0:T(8,128)(2,1)} %param.11) | copy-start | bytes 18874372
  208.3 110.4 %copy-start.3 = (bf16[512,512]{1,0:T(8,128)(2,1)S(1)}, bf16[512,512]{1,0:T(8,128)(2,1)}, u32[]{:S(2)}) copy-start(bf16[512,512]{1,0:T(8,128)(2,1)} %param.16) | copy-start | bytes 1572868
  208.3 110.4 %copy-start.4 = (f32[512]{0:T(512)S(1)}, f32[512]{0:T(512)}, u32[]{:S(2)}) copy-start(f32[512]{0:T(512)} %param.17) | copy-start | bytes 6148
Sparse Core Ops, SparseCore 0:
  25.0 183.2 all-gather.1
